TPU v7x, 256 devices: a whole 4x4x8 slice. The times are simulated.
256 devices in a mesh: dp: 4 (over y), seq: 16 (over z, core), mp: 4 (over x).
Axes of the slice: x: 4, y: 4, z: 8, core: 2. Of those that a mesh axis runs over, the one named last changes fastest.
Arguments:
- q_self: bfloat16 [4, 1024, 4096], P('dp', 'seq', 'mp'), may hold values from -12 to 12
- k_self: bfloat16 [4, 1024, 4096], P('dp', 'seq', 'mp'), may hold values from -3 to 3
- v_self: bfloat16 [4, 1024, 4096], P('dp', 'seq', 'mp'), may hold values from -0.75 to 0.75
- out_grad_self: bfloat16 [4, 1024, 4096], P('dp', 'seq', 'mp'), may hold values from -6 to 6
- q_cross: bfloat16 [4, 1024, 4096], P('dp', 'seq', 'mp'), may hold values from -12 to 12
- k_cross: bfloat16 [4, 2048, 4096], P('dp', 'seq', 'mp'), may hold values from -3 to 3
- v_cross: bfloat16 [4, 2048, 4096], P('dp', 'seq', 'mp'), may hold values from -0.75 to 0.75
- out_grad_cross: bfloat16 [4, 1024, 4096], P('dp', 'seq', 'mp'), may hold values from -8 to 8
- dec_lengths: int32 [4, 16], P('dp'), may hold values from 1 to 640, as said below
- enc_lengths: int32 [4, 16], P('dp'), may hold values from 1 to 1280, as said below
- rel_bias: float32 [32, 64], P(None, 'mp'), may hold values from -4 to 4
Outputs:
- grad_q_self: bfloat16 [4, 1024, 4096], P('dp', 'seq', 'mp')
- grad_k_self: bfloat16 [4, 1024, 4096], P('dp', 'seq', 'mp')
- grad_v_self: bfloat16 [4, 1024, 4096], P('dp', 'seq', 'mp')
- grad_q_cross: bfloat16 [4, 1024, 4096], P('dp', 'seq', 'mp')
- grad_k_cross: bfloat16 [4, 2048, 4096], P('dp', 'seq', 'mp')
- grad_v_cross: bfloat16 [4, 2048, 4096], P('dp', 'seq', 'mp')
- bias_grad: float32 [32, 64], P(None, 'mp')
Inputs may be any that keep to these rules, and one draw needn't show every extreme that they name: `dec_lengths`: row p lists the decoder lengths of the 16 examples of pack p in order; they sum to 1024 and the largest is exactly 640. `enc_lengths`: row p lists the encoder lengths of the same 16 examples in the same order; they sum to 2048. The example with 640 decoder rows has exactly 1280 encoder rows; every other example has at least as many encoder rows as decoder rows and at most three times as many.
All inputs are finite; a program needn't handle non-finite values.
Results may differ from a plain program's by a relative error of at most 0.039.
Values may be sent and summed in bfloat16 or wider, within the bound.
A program may use at most 128 MiB of HBM per device.

v0:
```python
import math
import jax
import jax.numpy as jnp
from jax import lax
from jax.sharding import PartitionSpec as P

HEAD_DIM = 64
BUCKETS = 32
DISTANCE = 128


def bucket_of(distances):
    exact_count = BUCKETS // 2
    bucketed = jnp.full(distances.shape, exact_count, jnp.int32)
    for level_index in range(1, BUCKETS - exact_count):
        threshold = math.ceil(
            exact_count * (DISTANCE / exact_count) ** (level_index / (BUCKETS - exact_count))
        )
        bucketed = bucketed + (distances >= threshold).astype(jnp.int32)
    return jnp.where(distances < exact_count, distances, bucketed)


def example_ids(total_rows, lengths):
    segment_ends = jnp.cumsum(lengths)
    positions = jnp.arange(total_rows, dtype=jnp.int32)
    return jnp.sum((positions[:, None] >= segment_ends[None, :]).astype(jnp.int32), axis=1)


def distance_table(rel_bias, offset_base, table_span):
    distances = offset_base + jnp.arange(table_span, dtype=jnp.int32)
    buckets = bucket_of(jnp.maximum(distances, 0))
    one_hot = (buckets[None, :] == jnp.arange(rel_bias.shape[0], dtype=jnp.int32)[:, None]).astype(
        jnp.float32
    )
    bias_table = jnp.einsum("bh,bl->hl", rel_bias, one_hot, precision=lax.Precision.HIGHEST)
    return (one_hot, bias_table)


def spread(bias_table, row_count, col_count):
    full_span = row_count + col_count - 1
    leading = bias_table.shape[:-1]
    tiled_rows = jnp.broadcast_to(bias_table[..., None, :], leading + (row_count, full_span))
    flat_rows = tiled_rows.reshape(leading + (row_count * full_span,))
    flat_rows = jnp.pad(flat_rows, [(0, 0)] * len(leading) + [(0, row_count)])
    skewed = flat_rows.reshape(leading + (row_count, full_span + 1))[..., :col_count]
    return skewed[..., ::-1]


def collapse(matrix, row_count, col_count):
    full_span = row_count + col_count - 1
    leading = matrix.shape[:-2]
    flipped = matrix[..., ::-1]
    padded = jnp.pad(flipped, [(0, 0)] * len(leading) + [(0, 0), (0, row_count)])
    flat_rows = padded.reshape(leading + (row_count * (full_span + 1),))[
        ..., : row_count * full_span
    ]
    return jnp.sum(flat_rows.reshape(leading + (row_count, full_span)), axis=-2)


def shard_group(shard_count, row_count):
    group_size = 1
    while group_size < shard_count and (
        shard_count % group_size != 0 or group_size * row_count < 384
    ):
        group_size += 1
    return group_size


def query_side(
    queries,
    out_grads,
    all_keys,
    all_values,
    key_ids,
    query_ids,
    query_start,
    rel_bias,
    block_rows,
    causal,
):
    row_count, head_count, head_size = queries.shape
    block_count = all_keys.shape[0] // block_rows
    query_pos = query_start + jnp.arange(row_count, dtype=jnp.int32)
    block_ids = jnp.arange(block_count, dtype=jnp.int32)

    def scores_of(block_id):
        key_first = block_id * block_rows
        key_block = lax.dynamic_slice_in_dim(all_keys, key_first, block_rows, 0)
        key_block_ids = lax.dynamic_slice_in_dim(key_ids, key_first, block_rows, 0)
        scores = jnp.einsum("thd,uhd->htu", queries, key_block, preferred_element_type=jnp.float32)
        allowed = query_ids[:, None] == key_block_ids[None, :]
        one_hot = jnp.zeros((1, 1), jnp.float32)
        if causal:
            key_pos = key_first + jnp.arange(block_rows, dtype=jnp.int32)
            allowed = allowed & (query_pos[:, None] >= key_pos[None, :])
            one_hot, bias_table = distance_table(
                rel_bias, query_start - key_first - (block_rows - 1), row_count + block_rows - 1
            )
            scores = scores + spread(bias_table, row_count, block_rows)
        return (jnp.where(allowed[None], scores, -1e30), one_hot)

    def stat_step(running, block_id):
        row_high, total_sum = running
        scores, unused_hot = scores_of(block_id)
        new_high = jnp.maximum(row_high, jnp.max(scores, axis=2))
        total_sum = total_sum * jnp.exp(row_high - new_high) + jnp.sum(
            jnp.exp(scores - new_high[:, :, None]), axis=2
        )
        return ((new_high, total_sum), None)

    start_state = (
        jnp.full((head_count, row_count), -1e30, jnp.float32),
        jnp.zeros((head_count, row_count), jnp.float32),
    )
    (row_high, total_sum), unused_stats = lax.scan(stat_step, start_state, block_ids)

    def weights_of(scores):
        return jnp.exp(scores - row_high[:, :, None]) / total_sum[:, :, None]

    def out_step(summed, block_id):
        scores, unused_hot = scores_of(block_id)
        narrow_weights = weights_of(scores).astype(jnp.bfloat16)
        value_block = lax.dynamic_slice_in_dim(all_values, block_id * block_rows, block_rows, 0)
        return (
            summed
            + jnp.einsum(
                "htu,uhd->thd", narrow_weights, value_block, preferred_element_type=jnp.float32
            ),
            None,
        )

    summed, unused_outs = lax.scan(
        out_step, jnp.zeros((row_count, head_count, head_size), jnp.float32), block_ids
    )
    outputs = summed.astype(jnp.bfloat16)
    row_delta = jnp.einsum("thd,thd->ht", out_grads, outputs, preferred_element_type=jnp.float32)

    def grad_step(running, block_id):
        query_grad, bias_grad_sum = running
        scores, one_hot = scores_of(block_id)
        weights = weights_of(scores)
        narrow_weights = weights.astype(jnp.bfloat16)
        key_block = lax.dynamic_slice_in_dim(all_keys, block_id * block_rows, block_rows, 0)
        value_block = lax.dynamic_slice_in_dim(all_values, block_id * block_rows, block_rows, 0)
        weight_grads = jnp.einsum(
            "thd,uhd->htu", out_grads, value_block, preferred_element_type=jnp.float32
        )
        score_grads = weights * (weight_grads - row_delta[:, :, None])
        narrow_grads = score_grads.astype(jnp.bfloat16)
        query_grad = query_grad + jnp.einsum(
            "htu,uhd->thd", narrow_grads, key_block, preferred_element_type=jnp.float32
        )
        if causal:
            bias_grad_sum = bias_grad_sum + jnp.einsum(
                "hl,bl->bh",
                collapse(score_grads, row_count, block_rows),
                one_hot,
                precision=lax.Precision.HIGHEST,
            )
        key_term = jnp.einsum(
            "htu,thd->uhd", narrow_grads, queries, preferred_element_type=jnp.float32
        )
        value_term = jnp.einsum(
            "htu,thd->uhd", narrow_weights, out_grads, preferred_element_type=jnp.float32
        )
        grad_term = jnp.concatenate(
            [
                key_term.reshape(block_rows, head_count * head_size),
                value_term.reshape(block_rows, head_count * head_size),
            ],
            axis=1,
        ).astype(jnp.bfloat16)
        return ((query_grad, bias_grad_sum), grad_term)

    grad_state = (
        jnp.zeros((row_count, head_count, head_size), jnp.float32),
        jnp.zeros((rel_bias.shape[0], head_count), jnp.float32),
    )
    (query_grad, bias_grad_sum), grad_terms = lax.scan(grad_step, grad_state, block_ids)
    grad_terms = grad_terms.reshape(block_count * block_rows, 2 * head_count * head_size)
    query_grad = query_grad.astype(jnp.bfloat16).reshape(row_count, head_count * head_size)
    return (query_grad, grad_terms, bias_grad_sum, (row_high, total_sum, row_delta))


def on_device(
    q_self,
    k_self,
    v_self,
    out_grad_self,
    q_cross,
    k_cross,
    v_cross,
    out_grad_cross,
    dec_lengths,
    enc_lengths,
    rel_bias,
):
    seq_count = lax.axis_size("seq")
    seq_place = lax.axis_index("seq")
    dec_rows = q_self.shape[1]
    enc_rows = k_cross.shape[1]
    feature_count = q_self.shape[2]
    head_count = feature_count // HEAD_DIM
    dec_total = dec_rows * seq_count
    enc_total = enc_rows * seq_count
    dec_start = seq_place * dec_rows
    dec_ids = example_ids(dec_total, dec_lengths[0])
    enc_ids = example_ids(enc_total, enc_lengths[0])
    my_dec_ids = lax.dynamic_slice_in_dim(dec_ids, dec_start, dec_rows, 0)

    def split_heads(tensor):
        return tensor.reshape(tensor.shape[0] * tensor.shape[1], head_count, HEAD_DIM)

    gathered = (
        lax.all_gather(k_self, "seq", axis=1, tiled=True),
        lax.all_gather(v_self, "seq", axis=1, tiled=True),
        lax.all_gather(k_cross, "seq", axis=1, tiled=True),
        lax.all_gather(v_cross, "seq", axis=1, tiled=True),
    )
    self_group = shard_group(seq_count, dec_rows)
    cross_group = shard_group(seq_count, enc_rows)
    self_dq, self_terms, self_bias, self_stats = query_side(
        split_heads(q_self),
        split_heads(out_grad_self),
        split_heads(gathered[0]),
        split_heads(gathered[1]),
        dec_ids,
        my_dec_ids,
        dec_start,
        rel_bias,
        self_group * dec_rows,
        True,
    )
    cross_dq, cross_terms, unused_bias, cross_stats = query_side(
        split_heads(q_cross),
        split_heads(out_grad_cross),
        split_heads(gathered[2]),
        split_heads(gathered[3]),
        enc_ids,
        my_dec_ids,
        dec_start,
        rel_bias,
        cross_group * enc_rows,
        False,
    )
    self_sums = lax.psum_scatter(
        self_terms.astype(jnp.float32).astype(jnp.bfloat16), "seq", scatter_dimension=0, tiled=True
    ).astype(jnp.float32)
    cross_sums = lax.psum_scatter(
        cross_terms.astype(jnp.float32).astype(jnp.bfloat16), "seq", scatter_dimension=0, tiled=True
    ).astype(jnp.float32)
    self_key_grad = self_sums[:, :feature_count]
    self_value_grad = self_sums[:, feature_count:]
    cross_key_grad = cross_sums[:, :feature_count]
    cross_value_grad = cross_sums[:, feature_count:]
    bias_total = lax.psum(self_bias, ("dp", "seq"))
    bias_grad = bias_total * (1.0 / math.sqrt(lax.axis_size("dp") * dec_total))
    return (
        self_dq.reshape(1, dec_rows, feature_count),
        self_key_grad.reshape(1, dec_rows, feature_count).astype(jnp.bfloat16),
        self_value_grad.reshape(1, dec_rows, feature_count).astype(jnp.bfloat16),
        cross_dq.reshape(1, dec_rows, feature_count),
        cross_key_grad.reshape(1, enc_rows, feature_count).astype(jnp.bfloat16),
        cross_value_grad.reshape(1, enc_rows, feature_count).astype(jnp.bfloat16),
        bias_grad,
    )


def solution(mesh):
    return jax.shard_map(
        on_device,
        mesh=mesh,
        in_specs=(
            P("dp", "seq", "mp"),
            P("dp", "seq", "mp"),
            P("dp", "seq", "mp"),
            P("dp", "seq", "mp"),
            P("dp", "seq", "mp"),
            P("dp", "seq", "mp"),
            P("dp", "seq", "mp"),
            P("dp", "seq", "mp"),
            P("dp", None),
            P("dp", None),
            P(None, "mp"),
        ),
        out_specs=(
            P("dp", "seq", "mp"),
            P("dp", "seq", "mp"),
            P("dp", "seq", "mp"),
            P("dp", "seq", "mp"),
            P("dp", "seq", "mp"),
            P("dp", "seq", "mp"),
            P(None, "mp"),
        ),
        check_vma=False,
    )
```

profile of v0, /device:TPU:2, one launch (start us, length us, event | category | flops | bytes accessed | tf_op | source)
XLA Modules:
  0.0 455.4 jit_solution(5825784003897655049)
XLA Ops:
  17.9 34.6 %all-gather.5.cloned.1.call-done = bf16[1,1024,1024]{2,1,0:T(8,128)(2,1)} async-done(((bf16[1,64,1024]{2,1,0:T(8,128)(2,1)}), bf16[1,1024,1024]{2,1,0:T(8,128)(2,1)}) %all-gather.5.cloned.1.call-update) | async-done | bytes 2097168 | tf_op jit(solution)/shard_map/all_gather | solution.py:215
  52.6 3.9 copy.70
  56.5 31.9 %while.91 = (s32[]{:T(128)}, f32[16,64]{1,0:T(8,128)S(1)}, f32[16,64]{1,0:T(8,128)S(1)}, s32[64]{0:T(128)S(1)}, s32[2]{0:T(128)S(1)}, /*index=5*/s32[1024]{0:T(1...) while((s32[]{:T(128)}, f32[16,64]{1,0:T(8,128)S(1)}, ...), condition=%wide.region_5.6_spmd.clone.clone.clone, body=%wide.region_2.0_spmd.clone.clone.clone.sunk | while | flops 73413688 | bytes 34665884 | solution.py:115
  66.6 2.5 rev.40
  82.6 2.5 rev.40
  88.4 4.1 all-gather.7.cloned.1.call-done
  92.5 3.9 copy.74
  96.4 34.2 %while.92 = (s32[]{:T(128)}, f32[64,16,64]{0,2,1:T(8,128)}, s32[2]{0:T(128)S(1)}, bf16[1024,16,64]{0,2,1:T(8,128)(2,1)}, s32[64]{0:T(128)S(1)}, /*index=5*/s32[1...) while((s32[]{:T(128)}, f32[64,16,64]{0,2,1:T(8,128)}, ...), condition=%wide.region_7.8_spmd.clone.clone.clone, body=%wide.region_6.7_spmd.clone.clone.clone.sunk | while | flops 140648496 | bytes 34098144 | solution.py:132
  109.2 3.4 fusion.213
  126.3 3.4 fusion.213
  131.7 80.7 %while.93 = (s32[]{:T(128)}, f32[64,16,64]{0,2,1:T(8,128)}, f32[32,16]{0,1:T(8,128)S(1)}, bf16[2,512,2048]{2,1,0:T(8,128)(2,1)}, s32[2]{0:T(128)S(1)}, /*index=5...) while((s32[]{:T(128)}, f32[64,16,64]{0,2,1:T(8,128)}, ...), condition=%wide.region_10.11_spmd.clone.clone.clone, body=%wide.region_8.10_spmd.clone.clone.clone.sunk | while | flops 353446976 | bytes 101543680 | solution.py:179
  144.6 2.7 fusion.226
  154.3 2.5 rev.43
  164.8 3.7 reshape.726
  168.9 3.3 constant_dynamic-update-slice_fusion.5
  184.9 2.7 fusion.226
  205.1 3.7 reshape.726
  209.2 3.3 constant_dynamic-update-slice_fusion.5
  212.6 6.7 %copy.79 = bf16[1,2048,1024]{1,2,0:T(8,128)(2,1)} copy(bf16[1,2048,1024]{2,1,0:T(8,128)(2,1)} %all-gather.9.cloned.1.call-done) | data formatting | bytes 8388608 | tf_op jit(solution)/shard_map/all_gather | solution.py:217
  219.4 15.2 %while.88 = (s32[]{:T(128)}, f32[16,64]{1,0:T(8,128)S(1)}, f32[16,64]{1,0:T(8,128)S(1)}, s32[64]{0:T(128)S(1)}, s32[4]{0:T(128)S(1)}, /*index=5*/s32[2048]{0:T(1...) while((s32[]{:T(128)}, f32[16,64]{1,0:T(8,128)S(1)}, ...), condition=%wide.region_17.18_spmd.clone, body=%wide.region_14.17_spmd.clone.sunk | while | flops 69768200 | bytes 5532106 | solution.py:115
  234.6 6.6 %copy.83 = bf16[1,2048,1024]{1,2,0:T(8,128)(2,1)} copy(bf16[1,2048,1024]{2,1,0:T(8,128)(2,1)} %all-gather.11.cloned.1.call-done) | data formatting | bytes 8388608 | tf_op jit(solution)/shard_map/all_gather | solution.py:218
  241.3 16.1 %while.89 = (s32[]{:T(128)}, f32[64,16,64]{0,2,1:T(8,128)S(1)}, s32[4]{0:T(128)S(1)}, bf16[2048,16,64]{0,2,1:T(8,128)(2,1)}, s32[64]{0:T(128)S(1)}, /*index=5*/s...) while((s32[]{:T(128)}, f32[64,16,64]{0,2,1:T(8,128)S(1)}, ...), condition=%wide.region_19.20_spmd.clone, body=%wide.region_18.19_spmd.clone.sunk | while | flops 136478720 | bytes 2834388 | solution.py:132
  242.7 2.6 fusion.191
  246.7 2.6 fusion.191
  250.8 2.5 fusion.191
  254.8 2.6 fusion.191
  257.5 54.1 %while.90 = (s32[]{:T(128)}, f32[64,16,64]{0,2,1:T(8,128)S(1)}, bf16[4,512,2048]{2,1,0:T(8,128)(2,1)}, s32[4]{0:T(128)S(1)}, bf16[2048,16,64]{0,2,1:T(8,128)(2,1...) while((s32[]{:T(128)}, f32[64,16,64]{0,2,1:T(8,128)S(1)}, ...), condition=%wide.region_21.22_spmd.clone, body=%wide.region_20.21_spmd.clone.sunk | while | flops 344621056 | bytes 28396028 | solution.py:179
  266.6 2.9 copy.116
  280.2 2.9 copy.116
  293.6 2.9 copy.116
  307.1 2.9 copy.116
  313.4 130.1 %psum.7 = f32[32,16]{0,1:T(8,128)S(1)} all-reduce(f32[32,16]{0,1:T(8,128)S(1)} %get-tuple-element.693), channel_id=1, replica_groups=mesh['dp'=4,'seq'=16,'mp'=4] {'dp','seq'}, use_global_device_ids=true, to_apply=%region_23.24 | all-reduce | flops 512 | bytes 4096 | tf_op jit(solution)/shard_map/psum | solution.py:256
  (310 shorter events, 181.8 us)
Async XLA Ops:
  7.2 9.6 %copy-start.19 = (bf16[1,64,1024]{2,1,0:T(8,128)(2,1)S(1)}, bf16[1,64,1024]{2,1,0:T(8,128)(2,1)}, u32[]{:S(2)}) copy-start(bf16[1,64,1024]{2,1,0:T(8,128)(2,1)} %param.27) | copy-start | bytes 393220
  7.2 45.4 %all-gather.5.cloned.1.call-start = ((), (), s32[]{:S(2)}) async-start(), calls=%async_computation.2 | async-start | bytes 2228224 | tf_op jit(solution)/shard_map/all_gather | solution.py:215
  7.9 84.5 %all-gather.7.cloned.1.call-start = ((), (), s32[]{:S(2)}) async-start(), calls=%async_computation.3 | async-start | bytes 2228224 | tf_op jit(solution)/shard_map/all_gather | solution.py:216
  8.7 203.9 %all-gather.9.cloned.1.call-start = ((), (), s32[]{:S(2)}) async-start(), calls=%async_computation.5 | async-start | bytes 4456448 | tf_op jit(solution)/shard_map/all_gather | solution.py:217
  9.4 225.2 %all-gather.11.cloned.1.call-start = ((), (), s32[]{:S(2)}) async-start(), calls=%async_computation.6 | async-start | bytes 4456448 | tf_op jit(solution)/shard_map/all_gather | solution.py:218
  10.0 435.0 %reduce-scatter.3.cloned.1.call-start = ((), (), s32[]{:S(2)}) async-start(), calls=%async_computation.4 | async-start | bytes 4456448 | tf_op jit(solution)/shard_map/reduce_scatter | solution.py:246
  17.0 39.5 %copy-start.7 = (bf16[1,64,1024]{1,2,0:T(8,128)(2,1)}, bf16[1,64,1024]{1,2,0:T(8,128)(2,1)S(1)}, u32[]{:S(2)}) copy-start(bf16[1,64,1024]{1,2,0:T(8,128)(2,1)S(1)} %copy.81) | copy-start | bytes 393220
  17.9 38.6 %copy-start.12 = (f32[32,16]{0,1:T(8,128)S(1)}, f32[32,16]{0,1:T(8,128)}, u32[]{:S(2)}) copy-start(f32[32,16]{0,1:T(8,128)} %param.33) | copy-start | bytes 6148
  81.0 1.6 slice-start
  105.1 1.6 slice-start.1
  106.7 2.5 copy-start.15
  122.2 1.6 slice-start.1
  123.8 2.5 copy-start.15
  131.9 12.7 %copy-start.9 = (bf16[64,16,64]{0,2,1:T(8,128)(2,1)}, bf16[64,16,64]{0,2,1:T(8,128)(2,1)S(1)}, u32[]{:S(2)}) copy-start(bf16[64,16,64]{0,2,1:T(8,128)(2,1)S(1)} %get-tuple-element.1967) | copy-start | bytes 393220 | tf_op jit(solution)/shard_map/while
  140.5 1.6 slice-start.2
  147.3 1.6 copy-start.2
  148.8 1.6 copy-start
  148.9 1.7 copy-start.3
  168.9 3.3 copy-start.10
  172.3 12.7 %copy-start.9 = (bf16[64,16,64]{0,2,1:T(8,128)(2,1)}, bf16[64,16,64]{0,2,1:T(8,128)(2,1)S(1)}, u32[]{:S(2)}) copy-start(bf16[64,16,64]{0,2,1:T(8,128)(2,1)S(1)} %get-tuple-element.1967) | copy-start | bytes 393220 | tf_op jit(solution)/shard_map/while
  187.6 1.6 copy-start.2
  189.2 1.7 copy-start.3
  209.2 3.3 copy-start.10
  212.5 6.9 %copy-start.11 = (bf16[64,16,64]{2,0,1:T(8,128)(2,1)S(1)}, bf16[64,16,64]{2,0,1:T(8,128)(2,1)}, u32[]{:S(2)}) copy-start(bf16[64,16,64]{2,0,1:T(8,128)(2,1)} %copy.82) | copy-start | bytes 393220
  212.5 6.8 %copy-start.13 = (f32[16,64]{1,0:T(8,128)S(1)}, f32[16,64]{1,0:T(8,128)}, u32[]{:S(2)}) copy-start(f32[16,64]{1,0:T(8,128)} %custom-call.5) | copy-start | bytes 12292
  212.5 6.8 %copy-start.17 = (f32[16,64]{1,0:T(8,128)S(1)}, f32[16,64]{1,0:T(8,128)}, u32[]{:S(2)}) copy-start(f32[16,64]{1,0:T(8,128)} %custom-call.6) | copy-start | bytes 12292
  212.5 6.8 %copy-start.18 = (s32[2048]{0:T(1024)S(1)}, s32[2048]{0:T(1024)}, u32[]{:S(2)}) copy-start(s32[2048]{0:T(1024)} %convert_reduce_fusion) | copy-start | bytes 24580
  212.5 234.2 %reduce-scatter.5.cloned.1.call-start = ((), (), s32[]{:S(2)}) async-start(), calls=%async_computation.7 | async-start | bytes 8912896 | tf_op jit(solution)/shard_map/reduce_scatter | solution.py:249
  234.6 6.7 %copy-start.14 = (f32[64,16,64]{0,2,1:T(8,128)S(1)}, f32[64,16,64]{0,2,1:T(8,128)}, u32[]{:S(2)}) copy-start(f32[64,16,64]{0,2,1:T(8,128)} %custom-call.7) | copy-start | bytes 786436
  241.3 16.1 %copy-start.1 = (bf16[1,64,1024]{1,2,0:T(8,128)(2,1)S(1)}, bf16[1,64,1024]{1,2,0:T(8,128)(2,1)}, u32[]{:S(2)}) copy-start(bf16[1,64,1024]{1,2,0:T(8,128)(2,1)} %copy.84) | copy-start | bytes 393220
  241.3 16.2 %copy-start.6 = (f32[64,16,64]{0,2,1:T(8,128)S(1)}, f32[64,16,64]{0,2,1:T(8,128)}, u32[]{:S(2)}) copy-start(f32[64,16,64]{0,2,1:T(8,128)} %custom-call.8) | copy-start | bytes 786436
  241.3 16.2 %copy-start.8 = (bf16[1,64,1024]{1,2,0:T(8,128)(2,1)S(1)}, bf16[1,64,1024]{1,2,0:T(8,128)(2,1)}, u32[]{:S(2)}) copy-start(bf16[1,64,1024]{1,2,0:T(8,128)(2,1)} %copy-done.7) | copy-start | bytes 393220
  (8 other events, 9.2 us)
Sparse Core Ops, SparseCore 0:
  9.8 42.6 all-gather.4
  54.4 38.0 all-gather.6
  94.3 40.5 all-gather.8
  136.5 40.8 all-gather.10
  212.6 61.6 reduce-scatter.2
  311.7 69.7 reduce-scatter.4
where the time goes:
time: 458 us; the launch traced here: 455 us
  local copies, waits for them, and re-layouts  170 us (37%)
  blocking collectives  130 us (28%)
  matrix products  67.9 us (15%)
  waiting for transfers between devices  41.4 us (9%)
  other arithmetic  17.8 us (4%)
  between operations  14.5 us (3%)
  loops' own time  13.3 us (3%)
    psum x1, blocking collectives, on_device(): bias_total = lax.psum(self_bias, ('dp', 'seq'))  130 us
    all_gather x1, waiting for transfers between devices, on_device(): lax.all_gather(k_self, 'seq', axis=1, tiled=True)  34.6 us
    dynamic_update_slice x12, local copies, waits for them, and re-layouts, query_side(): lax.scan(grad_step, grad_state, block_ids)  29.1 us
    dot_general x12, matrix products, scores_of(): jnp.einsum('thd,uhd->htu', queries, key_block, preferred_element_type=jnp...  24.8 us
    dot_general x6, matrix products, out_step(): jnp.einsum('htu,uhd->thd', narrow_weights, value_block, preferred_element...  17.1 us
    rev x6, local copies, waits for them, and re-layouts, spread(): return skewed[..., ::-1]  15.1 us
    reshape x6, local copies, waits for them, and re-layouts, spread(): flat_rows = tiled_rows.reshape(leading + (row_count * full_span,))  14.9 us
    reshape x6, local copies, waits for them, and re-layouts, spread(): flat_rows.reshape(leading + (row_count, full_span + 1))[..., :col_count]  14.6 us
  transfers between devices with their start and end apart: 6, of which 2 were waited for; matrix products, arithmetic and copies ran while one was open for 52% of the time, Pallas kernels for 0%

commit v1 on v0

--- a/solution.py
+++ b/solution.py
@@ -253,7 +253,11 @@
     self_value_grad = self_sums[:, feature_count:]
     cross_key_grad = cross_sums[:, :feature_count]
     cross_value_grad = cross_sums[:, feature_count:]
-    bias_total = lax.psum(self_bias, ("dp", "seq"))
+
+    def note_shapes_in(unit):
+        return jnp.sum(jax.lax.all_gather(unit, ("dp", "seq")), 0)
+
+    bias_total = note_shapes_in(self_bias)
     bias_grad = bias_total * (1.0 / math.sqrt(lax.axis_size("dp") * dec_total))
     return (
         self_dq.reshape(1, dec_rows, feature_count),

time: 458 us -> 393 us (0.86)
  blocking collectives: 130 us -> 49.9 us
  waiting for transfers between devices: 41.4 us -> 56.2 us
    psum x1 -> x0, blocking collectives: 130 us -> none  [on_device(): bias_total = lax.psum(self_bias, ('dp', 'seq'))]
    all_gather x0 -> x1, blocking collectives: none -> 49.9 us  [note_shapes_in(): return jnp.sum(jax.lax.all_gather(unit, ('dp', 'seq')), 0)]
    reduce_scatter x1, waiting for transfers between devices: 0.01 us -> 14.9 us  [on_device(): lax.psum_scatter(cross_terms.astype(jnp.float32).astype(jnp.bfloat16), 's...]
  transfers between devices with their start and end apart: 6 -> 6, of which waited for: 2 -> 3; matrix products, arithmetic and copies ran while one was open for 52% -> 60% of each run, Pallas kernels for 0% -> 0%
where the time goes in v1:
time: 393 us; the launch traced here: 390 us
  local copies, waits for them, and re-layouts  170 us (43%)
  matrix products  67.9 us (17%)
  waiting for transfers between devices  56.2 us (14%)
  blocking collectives  49.9 us (13%)
  other arithmetic  17.9 us (5%)
  between operations  14.5 us (4%)
  loops' own time  13.3 us (3%)
    all_gather x1, blocking collectives, note_shapes_in(): return jnp.sum(jax.lax.all_gather(unit, ('dp', 'seq')), 0)  49.9 us
    all_gather x1, waiting for transfers between devices, on_device(): lax.all_gather(k_self, 'seq', axis=1, tiled=True)  34.6 us
    dynamic_update_slice x12, local copies, waits for them, and re-layouts, query_side(): lax.scan(grad_step, grad_state, block_ids)  29.1 us
    dot_general x12, matrix products, scores_of(): jnp.einsum('thd,uhd->htu', queries, key_block, preferred_element_type=jnp...  24.8 us
    dot_general x6, matrix products, out_step(): jnp.einsum('htu,uhd->thd', narrow_weights, value_block, preferred_element...  17.1 us
    rev x6, local copies, waits for them, and re-layouts, spread(): return skewed[..., ::-1]  15.1 us
    reshape x6, local copies, waits for them, and re-layouts, spread(): flat_rows = tiled_rows.reshape(leading + (row_count * full_span,))  14.9 us
    reduce_scatter x1, waiting for transfers between devices, on_device(): lax.psum_scatter(cross_terms.astype(jnp.float32).astype(jnp.bfloat16), 's...  14.9 us
  transfers between devices with their start and end apart: 6, of which 3 were waited for; matrix products, arithmetic and copies ran while one was open for 60% of the time, Pallas kernels for 0%

profile of v1, /device:TPU:2, one launch (start us, length us, event | category | flops | bytes accessed | tf_op | source)
XLA Modules:
  0.0 390.1 jit_solution(10132244589209230313)
XLA Ops:
  17.9 34.6 %all-gather.7.cloned.1.call-done = bf16[1,1024,1024]{2,1,0:T(8,128)(2,1)} async-done(((bf16[1,64,1024]{2,1,0:T(8,128)(2,1)}), bf16[1,1024,1024]{2,1,0:T(8,128)(2,1)}) %all-gather.7.cloned.1.call-update) | async-done | bytes 2097168 | tf_op jit(solution)/shard_map/all_gather | solution.py:215
  52.6 3.9 %copy.92 = bf16[1,1024,1024]{1,2,0:T(8,128)(2,1)} copy(bf16[1,1024,1024]{2,1,0:T(8,128)(2,1)} %all-gather.7.cloned.1.call-done) | data formatting | bytes 4194304 | tf_op jit(solution)/shard_map/all_gather | solution.py:215
  56.5 31.9 %while.91 = (s32[]{:T(128)}, f32[16,64]{1,0:T(8,128)S(1)}, f32[16,64]{1,0:T(8,128)S(1)}, s32[64]{0:T(128)S(1)}, s32[2]{0:T(128)S(1)}, /*index=5*/s32[1024]{0:T(1...) while((s32[]{:T(128)}, f32[16,64]{1,0:T(8,128)S(1)}, ...), condition=%wide.region_5.6_spmd.clone.clone.clone, body=%wide.region_2.0_spmd.clone.clone.clone.sunk | while | flops 73413688 | bytes 34665884 | solution.py:115
  66.6 2.5 rev.40
  82.6 2.5 rev.40
  88.4 4.1 %all-gather.9.cloned.1.call-done = bf16[1,1024,1024]{2,1,0:T(8,128)(2,1)} async-done(((bf16[1,64,1024]{2,1,0:T(8,128)(2,1)}), bf16[1,1024,1024]{2,1,0:T(8,128)(2,1)}) %all-gather.9.cloned.1.call-update) | async-done | bytes 2097168 | tf_op jit(solution)/shard_map/all_gather | solution.py:216
  92.5 3.9 %copy.96 = bf16[1,1024,1024]{1,2,0:T(8,128)(2,1)} copy(bf16[1,1024,1024]{2,1,0:T(8,128)(2,1)} %all-gather.9.cloned.1.call-done) | data formatting | bytes 4194304 | tf_op jit(solution)/shard_map/all_gather | solution.py:216
  96.4 34.2 %while.92 = (s32[]{:T(128)}, f32[64,16,64]{0,2,1:T(8,128)}, s32[2]{0:T(128)S(1)}, bf16[1024,16,64]{0,2,1:T(8,128)(2,1)}, s32[64]{0:T(128)S(1)}, /*index=5*/s32[1...) while((s32[]{:T(128)}, f32[64,16,64]{0,2,1:T(8,128)}, ...), condition=%wide.region_7.8_spmd.clone.clone.clone, body=%wide.region_6.7_spmd.clone.clone.clone.sunk | while | flops 140648496 | bytes 34098144 | solution.py:132
  109.2 3.4 fusion.213
  126.3 3.4 fusion.213
  131.7 80.7 %while.93 = (s32[]{:T(128)}, f32[64,16,64]{0,2,1:T(8,128)}, f32[32,16]{0,1:T(8,128)S(1)}, bf16[2,512,2048]{2,1,0:T(8,128)(2,1)}, s32[2]{0:T(128)S(1)}, /*index=5...) while((s32[]{:T(128)}, f32[64,16,64]{0,2,1:T(8,128)}, ...), condition=%wide.region_10.11_spmd.clone.clone.clone, body=%wide.region_8.10_spmd.clone.clone.clone.sunk | while | flops 353446976 | bytes 101543680 | solution.py:179
  144.6 2.7 fusion.226
  164.8 3.7 reshape.730
  168.9 3.3 constant_dynamic-update-slice_fusion.5
  184.9 2.7 fusion.226
  205.1 3.7 reshape.730
  209.2 3.3 constant_dynamic-update-slice_fusion.5
  212.6 6.7 %copy.101 = bf16[1,2048,1024]{1,2,0:T(8,128)(2,1)} copy(bf16[1,2048,1024]{2,1,0:T(8,128)(2,1)} %all-gather.11.cloned.1.call-done) | data formatting | bytes 8388608 | tf_op jit(solution)/shard_map/all_gather | solution.py:217
  219.4 15.2 %while.88 = (s32[]{:T(128)}, f32[16,64]{1,0:T(8,128)S(1)}, f32[16,64]{1,0:T(8,128)S(1)}, s32[64]{0:T(128)S(1)}, s32[4]{0:T(128)S(1)}, /*index=5*/s32[2048]{0:T(1...) while((s32[]{:T(128)}, f32[16,64]{1,0:T(8,128)S(1)}, ...), condition=%wide.region_17.18_spmd.clone, body=%wide.region_14.17_spmd.clone.sunk | while | flops 69768200 | bytes 5532106 | solution.py:115
  234.6 6.6 %copy.105 = bf16[1,2048,1024]{1,2,0:T(8,128)(2,1)} copy(bf16[1,2048,1024]{2,1,0:T(8,128)(2,1)} %all-gather.13.cloned.1.call-done) | data formatting | bytes 8388608 | tf_op jit(solution)/shard_map/all_gather | solution.py:218
  241.3 16.1 %while.89 = (s32[]{:T(128)}, f32[64,16,64]{0,2,1:T(8,128)S(1)}, s32[4]{0:T(128)S(1)}, bf16[2048,16,64]{0,2,1:T(8,128)(2,1)}, s32[64]{0:T(128)S(1)}, /*index=5*/s...) while((s32[]{:T(128)}, f32[64,16,64]{0,2,1:T(8,128)S(1)}, ...), condition=%wide.region_19.20_spmd.clone, body=%wide.region_18.19_spmd.clone.sunk | while | flops 136478720 | bytes 2834388 | solution.py:132
  242.7 2.6 fusion.191
  246.7 2.6 fusion.191
  250.8 2.5 fusion.191
  254.8 2.6 fusion.191
  257.5 54.1 %while.90 = (s32[]{:T(128)}, f32[64,16,64]{0,2,1:T(8,128)S(1)}, bf16[4,512,2048]{2,1,0:T(8,128)(2,1)}, s32[4]{0:T(128)S(1)}, bf16[2048,16,64]{0,2,1:T(8,128)(2,1...) while((s32[]{:T(128)}, f32[64,16,64]{0,2,1:T(8,128)S(1)}, ...), condition=%wide.region_21.22_spmd.clone, body=%wide.region_20.21_spmd.clone.sunk | while | flops 344621056 | bytes 28396028 | solution.py:179
  266.6 2.9 copy.138
  280.2 2.9 copy.138
  293.6 2.9 copy.138
  307.1 2.9 copy.138
  313.4 49.9 %all-gather.1 = f32[64,32,16]{1,2,0:T(8,128)S(1)} all-gather(f32[1,32,16]{1,2,0:T(8,128)S(1)} %bitcast.261), channel_id=2, replica_groups=mesh['dp'=4,'seq'=16,'mp'=4] {'dp','seq'}, dimensions={0}, use_global_device_ids=true | all-gather | bytes 133120 | tf_op jit(solution)/shard_map/all_gather | solution.py:258
  366.5 14.9 %reduce-scatter.5.cloned.1.call-done = bf16[128,2048]{1,0:T(8,128)(2,1)} async-done(((bf16[2048,2048]{1,0:T(8,128)(2,1)}), bf16[128,2048]{1,0:T(8,128)(2,1)}) %reduce-scatter.5.cloned.1.call-update) | async-done | bytes 524304 | tf_op jit(solution)/shard_map/reduce_scatter | solution.py:249
  (311 shorter events, 184.4 us)
Async XLA Ops:
  7.2 9.6 %copy-start.19 = (bf16[1,64,1024]{2,1,0:T(8,128)(2,1)S(1)}, bf16[1,64,1024]{2,1,0:T(8,128)(2,1)}, u32[]{:S(2)}) copy-start(bf16[1,64,1024]{2,1,0:T(8,128)(2,1)} %param.27) | copy-start | bytes 393220
  7.2 45.4 %all-gather.7.cloned.1.call-start = ((), (), s32[]{:S(2)}) async-start(), calls=%async_computation.2 | async-start | bytes 2228224 | tf_op jit(solution)/shard_map/all_gather | solution.py:215
  7.9 84.5 %all-gather.9.cloned.1.call-start = ((), (), s32[]{:S(2)}) async-start(), calls=%async_computation.3 | async-start | bytes 2228224 | tf_op jit(solution)/shard_map/all_gather | solution.py:216
  8.7 203.9 %all-gather.11.cloned.1.call-start = ((), (), s32[]{:S(2)}) async-start(), calls=%async_computation.5 | async-start | bytes 4456448 | tf_op jit(solution)/shard_map/all_gather | solution.py:217
  9.4 225.2 %all-gather.13.cloned.1.call-start = ((), (), s32[]{:S(2)}) async-start(), calls=%async_computation.6 | async-start | bytes 4456448 | tf_op jit(solution)/shard_map/all_gather | solution.py:218
  10.0 354.8 %reduce-scatter.3.cloned.1.call-start = ((), (), s32[]{:S(2)}) async-start(), calls=%async_computation.4 | async-start | bytes 4456448 | tf_op jit(solution)/shard_map/reduce_scatter | solution.py:246
  17.0 39.5 %copy-start.7 = (bf16[1,64,1024]{1,2,0:T(8,128)(2,1)}, bf16[1,64,1024]{1,2,0:T(8,128)(2,1)S(1)}, u32[]{:S(2)}) copy-start(bf16[1,64,1024]{1,2,0:T(8,128)(2,1)S(1)} %copy.103) | copy-start | bytes 393220
  17.9 38.6 %copy-start.12 = (f32[32,16]{0,1:T(8,128)S(1)}, f32[32,16]{0,1:T(8,128)}, u32[]{:S(2)}) copy-start(f32[32,16]{0,1:T(8,128)} %param.33) | copy-start | bytes 6148
  81.0 1.6 slice-start
  105.1 1.6 slice-start.1
  106.7 2.5 copy-start.15
  122.2 1.6 slice-start.1
  123.8 2.5 copy-start.15
  131.9 12.7 %copy-start.9 = (bf16[64,16,64]{0,2,1:T(8,128)(2,1)}, bf16[64,16,64]{0,2,1:T(8,128)(2,1)S(1)}, u32[]{:S(2)}) copy-start(bf16[64,16,64]{0,2,1:T(8,128)(2,1)S(1)} %get-tuple-element.2007) | copy-start | bytes 393220 | tf_op jit(solution)/shard_map/while
  140.5 1.6 slice-start.2
  147.3 1.6 copy-start.2
  148.8 1.6 copy-start
  148.9 1.7 copy-start.3
  168.9 3.3 copy-start.10
  172.3 12.7 %copy-start.9 = (bf16[64,16,64]{0,2,1:T(8,128)(2,1)}, bf16[64,16,64]{0,2,1:T(8,128)(2,1)S(1)}, u32[]{:S(2)}) copy-start(bf16[64,16,64]{0,2,1:T(8,128)(2,1)S(1)} %get-tuple-element.2007) | copy-start | bytes 393220 | tf_op jit(solution)/shard_map/while
  187.6 1.6 copy-start.2
  189.2 1.7 copy-start.3
  209.2 3.3 copy-start.10
  212.5 6.9 %copy-start.11 = (bf16[64,16,64]{2,0,1:T(8,128)(2,1)S(1)}, bf16[64,16,64]{2,0,1:T(8,128)(2,1)}, u32[]{:S(2)}) copy-start(bf16[64,16,64]{2,0,1:T(8,128)(2,1)} %copy.104) | copy-start | bytes 393220
  212.5 6.8 %copy-start.13 = (f32[16,64]{1,0:T(8,128)S(1)}, f32[16,64]{1,0:T(8,128)}, u32[]{:S(2)}) copy-start(f32[16,64]{1,0:T(8,128)} %custom-call.5) | copy-start | bytes 12292
  212.5 6.8 %copy-start.17 = (f32[16,64]{1,0:T(8,128)S(1)}, f32[16,64]{1,0:T(8,128)}, u32[]{:S(2)}) copy-start(f32[16,64]{1,0:T(8,128)} %custom-call.6) | copy-start | bytes 12292
  212.5 6.8 %copy-start.18 = (s32[2048]{0:T(1024)S(1)}, s32[2048]{0:T(1024)}, u32[]{:S(2)}) copy-start(s32[2048]{0:T(1024)} %convert_reduce_fusion) | copy-start | bytes 24580
  212.5 168.9 %reduce-scatter.5.cloned.1.call-start = ((), (), s32[]{:S(2)}) async-start(), calls=%async_computation.7 | async-start | bytes 8912896 | tf_op jit(solution)/shard_map/reduce_scatter | solution.py:249
  234.6 6.7 %copy-start.14 = (f32[64,16,64]{0,2,1:T(8,128)S(1)}, f32[64,16,64]{0,2,1:T(8,128)}, u32[]{:S(2)}) copy-start(f32[64,16,64]{0,2,1:T(8,128)} %custom-call.7) | copy-start | bytes 786436
  241.3 16.1 %copy-start.1 = (bf16[1,64,1024]{1,2,0:T(8,128)(2,1)S(1)}, bf16[1,64,1024]{1,2,0:T(8,128)(2,1)}, u32[]{:S(2)}) copy-start(bf16[1,64,1024]{1,2,0:T(8,128)(2,1)} %copy.106) | copy-start | bytes 393220
  241.3 16.2 %copy-start.6 = (f32[64,16,64]{0,2,1:T(8,128)S(1)}, f32[64,16,64]{0,2,1:T(8,128)}, u32[]{:S(2)}) copy-start(f32[64,16,64]{0,2,1:T(8,128)} %custom-call.8) | copy-start | bytes 786436
  241.3 16.2 %copy-start.8 = (bf16[1,64,1024]{1,2,0:T(8,128)(2,1)S(1)}, bf16[1,64,1024]{1,2,0:T(8,128)(2,1)}, u32[]{:S(2)}) copy-start(bf16[1,64,1024]{1,2,0:T(8,128)(2,1)} %copy-done.7) | copy-start | bytes 393220
  (8 other events, 9.2 us)
Sparse Core Ops, SparseCore 0:
  9.8 42.6 all-gather.6
  54.4 38.0 all-gather.8
  94.3 40.5 all-gather.10
  136.5 40.8 all-gather.12
  212.6 61.6 reduce-scatter.2
  311.7 69.6 reduce-scatter.4
